TPU v7x, 32 devices: a whole 2x2x4 slice. The times are simulated.
32 devices in a mesh: dp: 8 (over z, y), tensor: 4 (over x, core).
Axes of the slice: x: 2, y: 2, z: 4, core: 2. Of those that a mesh axis runs over, the one named last changes fastest.
Arguments:
- tokens: bfloat16 [16384, 1536], P(('dp', 'tensor')), may hold values from -6 to 6
- segments: int32 [16384], P('dp'), may hold values from 0 to 3, as said below
- positions: int32 [16384], P('dp'), may hold values from 0 to 2044, as said below
- norm_attn: float32 [1536], replicated, may hold values from 0.1 to 1.9
- w_query: bfloat16 [1536, 1536], P(None, 'tensor'), may hold values from -0.15625 to 0.15625
- key_weight: bfloat16 [1536, 768], P(None, 'tensor'), may hold values from -0.15625 to 0.15625
- value_weight: bfloat16 [1536, 768], P(None, 'tensor'), may hold values from -0.15625 to 0.15625
- w_out: bfloat16 [1536, 1536], P('tensor'), may hold values from -1.5 to 1.5
- norm_mlp: float32 [1536], replicated, may hold values from 0.1 to 1.9
- w_gate: bfloat16 [1536, 4096], P(None, 'tensor'), may hold values from -0.15625 to 0.15625
- w_up: bfloat16 [1536, 4096], P(None, 'tensor'), may hold values from -0.15625 to 0.15625
- w_down: bfloat16 [4096, 1536], P('tensor'), may hold values from -0.09375 to 0.09375
- cotangent: bfloat16 [16384, 1536], P(('dp', 'tensor')), may hold values from -6 to 6
Outputs:
- output: bfloat16 [16384, 1536], P(('dp', 'tensor'))
- grad_tokens: float32 [16384, 1536], P(('dp', 'tensor'))
- grad_norm_attn: float32 [1536], replicated
- grad_w_query: float32 [1536, 1536], P(None, 'tensor')
- grad_w_key: float32 [1536, 768], P(None, 'tensor')
- grad_w_value: float32 [1536, 768], P(None, 'tensor')
- grad_w_out: float32 [1536, 1536], P('tensor')
- grad_norm_mlp: float32 [1536], replicated
- grad_w_gate: float32 [1536, 4096], P(None, 'tensor')
- grad_w_up: float32 [1536, 4096], P(None, 'tensor')
- grad_w_down: float32 [4096, 1536], P('tensor')
Inputs may be any that keep to these rules, and one draw needn't show every extreme that they name: `segments`: within each sequence of 2048 tokens the document numbers never fall, start at 0 and end at 3, each document one token or more. `positions`: each token's position within its document, 0 at the document's first token; the first sequence holds a document of 2045 tokens.
All inputs are finite; a program needn't handle non-finite values.
Results may differ from a plain program's by a relative error of at most 0.018.
Values may be sent and summed in bfloat16 or wider, within the bound.
A program may use at most 256 MiB of HBM per device.

v0:
```python
import math
import jax
import jax.numpy as jnp
from jax import lax
from jax.sharding import PartitionSpec as P

HEAD_SIZE = 96
epsilon = 1e-05
rope_base = 100000.0
masked_value = -1e30


def angle_tables(positions, width):
    middle = width // 2
    freq_steps = jnp.arange(middle, dtype=jnp.float32)
    inverse = jnp.exp(freq_steps * (-2.0 * math.log(rope_base) / width))
    angles = positions.astype(jnp.float32)[:, None] * inverse[None, :]
    return (jnp.cos(angles)[:, None, :], jnp.sin(angles)[:, None, :])


def apply_rotary(values, cosine_lookup, sine_lookup):
    middle = values.shape[-1] // 2
    front, second = (values[..., :middle], values[..., middle:])
    return jnp.concatenate(
        [
            front * cosine_lookup - second * sine_lookup,
            second * cosine_lookup + front * sine_lookup,
        ],
        axis=-1,
    )


def rotate_back(grads_in, cosine_lookup, sine_lookup):
    middle = grads_in.shape[-1] // 2
    front, second = (grads_in[..., :middle], grads_in[..., middle:])
    return jnp.concatenate(
        [
            front * cosine_lookup + second * sine_lookup,
            second * cosine_lookup - front * sine_lookup,
        ],
        axis=-1,
    )


def rms_inverse(values):
    return lax.rsqrt(jnp.mean(values * values, axis=-1, keepdims=True) + epsilon)


def norm_back(grad_normed, gain, unit_rows, inverse):
    scaled = grad_normed * gain
    return inverse * (scaled - unit_rows * jnp.mean(scaled * unit_rows, axis=-1, keepdims=True))


def contract_rows(left, right):
    return lax.dot_general(
        left, right, (((0,), (0,)), ((), ())), preferred_element_type=jnp.float32
    )


def contract_cols(left, right):
    return lax.dot_general(
        left, right, (((1,), (1,)), ((), ())), preferred_element_type=jnp.float32
    )


def block_scores(query_block, heads_of_key, allowed, score_scale):
    scores = (
        jnp.einsum("qgrd,kgd->grqk", query_block, heads_of_key, preferred_element_type=jnp.float32)
        * score_scale
    )
    return jnp.where(allowed[None, None], scores, masked_value)


def body(
    tokens,
    segments,
    positions,
    norm_attn,
    w_query,
    key_weight,
    value_weight,
    w_out,
    norm_mlp,
    w_gate,
    w_up,
    w_down,
    cotangent,
):
    sequence_length = segments.shape[0]
    q_heads = w_query.shape[1] // HEAD_SIZE
    kv_heads = key_weight.shape[1] // HEAD_SIZE
    head_repetitions = q_heads // kv_heads
    score_scale = 1.0 / math.sqrt(HEAD_SIZE)
    rows_per_block = min(512, sequence_length)
    block_total = sequence_length // rows_per_block
    cosine_lookup, sine_lookup = angle_tables(positions, HEAD_SIZE)
    indices = jnp.arange(sequence_length, dtype=jnp.int32)
    seg_blocks = segments.reshape(block_total, rows_per_block)
    index_blocks = indices.reshape(block_total, rows_per_block)
    inputs = tokens.astype(jnp.float32)
    inverse_one = rms_inverse(inputs)
    unit_one = inputs * inverse_one
    first_normalized = (unit_one * norm_attn).astype(jnp.bfloat16)
    attn_in = lax.all_gather(first_normalized, "tensor", axis=0, tiled=True)
    query_proj = jnp.dot(attn_in, w_query, preferred_element_type=jnp.float32).reshape(
        sequence_length, q_heads, HEAD_SIZE
    )
    key_proj = jnp.dot(attn_in, key_weight, preferred_element_type=jnp.float32).reshape(
        sequence_length, kv_heads, HEAD_SIZE
    )
    query_rows = apply_rotary(query_proj, cosine_lookup, sine_lookup).astype(jnp.bfloat16)
    heads_of_key = apply_rotary(key_proj, cosine_lookup, sine_lookup).astype(jnp.bfloat16)
    heads_of_value = (
        jnp.dot(attn_in, value_weight, preferred_element_type=jnp.float32)
        .astype(jnp.bfloat16)
        .reshape(sequence_length, kv_heads, HEAD_SIZE)
    )
    blocks_of_query = query_rows.reshape(
        block_total, rows_per_block, kv_heads, head_repetitions, HEAD_SIZE
    )

    def attend(member):
        query_block, rows_seg, rows_idx = member
        allowed = (rows_seg[:, None] == segments[None, :]) & (indices[None, :] <= rows_idx[:, None])
        scores = block_scores(query_block, heads_of_key, allowed, score_scale)
        row_peak = jnp.max(scores, axis=-1, keepdims=True)
        weights = jnp.exp(scores - row_peak)
        totals = jnp.sum(weights, axis=-1, keepdims=True)
        weights_low = (weights / totals).astype(jnp.bfloat16)
        mixed_heads = jnp.einsum(
            "grqk,kgd->qgrd", weights_low, heads_of_value, preferred_element_type=jnp.float32
        )
        return (mixed_heads.astype(jnp.bfloat16), row_peak[..., 0] + jnp.log(totals[..., 0]))

    attended, log_totals = lax.map(attend, (blocks_of_query, seg_blocks, index_blocks))
    attended = attended.reshape(sequence_length, q_heads * HEAD_SIZE)
    row_slice = attended
    attn_out = lax.psum_scatter(
        jnp.dot(row_slice, w_out, preferred_element_type=jnp.float32),
        "tensor",
        scatter_dimension=0,
        tiled=True,
    )
    hidden_one = inputs + attn_out
    inverse_two = rms_inverse(hidden_one)
    unit_two = hidden_one * inverse_two
    normed_two = (unit_two * norm_mlp).astype(jnp.bfloat16)
    mlp_in = lax.all_gather(normed_two, "tensor", axis=0, tiled=True)
    gate_proj = jnp.dot(mlp_in, w_gate, preferred_element_type=jnp.float32)
    up_proj = jnp.dot(mlp_in, w_up, preferred_element_type=jnp.float32)
    sigmoid_gate = jax.nn.sigmoid(gate_proj)
    activated = gate_proj * sigmoid_gate
    hidden = (activated * up_proj).astype(jnp.bfloat16)
    row_slice = hidden
    mlp_out = lax.psum_scatter(
        jnp.dot(row_slice, w_down, preferred_element_type=jnp.float32).astype(jnp.bfloat16),
        "tensor",
        scatter_dimension=0,
        tiled=True,
    ).astype(jnp.float32)
    output = (hidden_one + mlp_out).astype(jnp.bfloat16)
    grad_out = lax.all_gather(cotangent, "tensor", axis=0, tiled=True)
    grad_w_down = contract_rows(hidden, grad_out)
    grad_hidden = contract_cols(grad_out, w_down)
    grad_gate = (
        grad_hidden * up_proj * sigmoid_gate * (1.0 + gate_proj * (1.0 - sigmoid_gate))
    ).astype(jnp.bfloat16)
    grad_upper = (grad_hidden * activated).astype(jnp.bfloat16)
    grad_w_gate = contract_rows(mlp_in, grad_gate)
    grad_w_up = contract_rows(mlp_in, grad_upper)
    grad_normed_two = lax.psum_scatter(
        contract_cols(grad_gate, w_gate) + contract_cols(grad_upper, w_up),
        "tensor",
        scatter_dimension=0,
        tiled=True,
    )
    grad_norm_mlp = jnp.sum(grad_normed_two * unit_two, axis=0)
    grad_hidden_one = cotangent.astype(jnp.float32) + norm_back(
        grad_normed_two, norm_mlp, unit_two, inverse_two
    )
    grad_attn_rows = lax.all_gather(
        grad_hidden_one.astype(jnp.bfloat16), "tensor", axis=0, tiled=True
    )
    grad_w_out = contract_rows(attended, grad_attn_rows)
    grad_attended = contract_cols(grad_attn_rows, w_out).astype(jnp.bfloat16)
    grad_blocks = grad_attended.reshape(
        block_total, rows_per_block, kv_heads, head_repetitions, HEAD_SIZE
    )

    def attend_back(running, member):
        query_block, grad_block, rows_seg, rows_idx, log_block = member
        allowed = (rows_seg[:, None] == segments[None, :]) & (indices[None, :] <= rows_idx[:, None])
        scores = block_scores(query_block, heads_of_key, allowed, score_scale)
        weights = jnp.exp(scores - log_block[..., None])
        grad_weights = jnp.einsum(
            "qgrd,kgd->grqk", grad_block, heads_of_value, preferred_element_type=jnp.float32
        )
        inner_sum = jnp.sum(weights * grad_weights, axis=-1, keepdims=True)
        grad_scores = (weights * (grad_weights - inner_sum)).astype(jnp.bfloat16)
        grad_query = (
            jnp.einsum(
                "grqk,kgd->qgrd", grad_scores, heads_of_key, preferred_element_type=jnp.float32
            )
            * score_scale
        )
        grad_keys = (
            running[0]
            + jnp.einsum(
                "grqk,qgrd->kgd", grad_scores, query_block, preferred_element_type=jnp.float32
            )
            * score_scale
        )
        grad_values = running[1] + jnp.einsum(
            "grqk,qgrd->kgd",
            weights.astype(jnp.bfloat16),
            grad_block,
            preferred_element_type=jnp.float32,
        )
        return ((grad_keys, grad_values), grad_query)

    zero_state = jnp.zeros((sequence_length, kv_heads, HEAD_SIZE), jnp.float32)
    (grad_keys, grad_values), grad_queries = lax.scan(
        attend_back,
        (zero_state, zero_state),
        (blocks_of_query, grad_blocks, seg_blocks, index_blocks, log_totals),
    )
    grad_queries = grad_queries.reshape(sequence_length, q_heads, HEAD_SIZE)
    grad_q_proj = (
        rotate_back(grad_queries, cosine_lookup, sine_lookup)
        .reshape(sequence_length, q_heads * HEAD_SIZE)
        .astype(jnp.bfloat16)
    )
    grad_k_proj = (
        rotate_back(grad_keys, cosine_lookup, sine_lookup)
        .reshape(sequence_length, kv_heads * HEAD_SIZE)
        .astype(jnp.bfloat16)
    )
    grad_v_proj = grad_values.reshape(sequence_length, kv_heads * HEAD_SIZE).astype(jnp.bfloat16)
    grad_w_query = contract_rows(attn_in, grad_q_proj)
    grad_w_key = contract_rows(attn_in, grad_k_proj)
    grad_w_value = contract_rows(attn_in, grad_v_proj)
    grad_normed_one = lax.psum_scatter(
        (
            contract_cols(grad_q_proj, w_query)
            + contract_cols(grad_k_proj, key_weight)
            + contract_cols(grad_v_proj, value_weight)
        ).astype(jnp.bfloat16),
        "tensor",
        scatter_dimension=0,
        tiled=True,
    ).astype(jnp.float32)
    grad_norm_attn = jnp.sum(grad_normed_one * unit_one, axis=0)
    grad_tokens = grad_hidden_one + norm_back(grad_normed_one, norm_attn, unit_one, inverse_one)
    grad_norm_attn, grad_norm_mlp = lax.psum((grad_norm_attn, grad_norm_mlp), ("dp", "tensor"))
    grad_w_query, grad_w_key, grad_w_value, grad_w_out, grad_w_gate, grad_w_up, grad_w_down = (
        lax.psum(grad_w_query.astype(jnp.bfloat16), "dp").astype(jnp.float32),
        lax.psum(grad_w_key.astype(jnp.bfloat16), "dp").astype(jnp.float32),
        lax.psum(grad_w_value.astype(jnp.bfloat16), "dp").astype(jnp.float32),
        lax.psum(grad_w_out.astype(jnp.bfloat16), "dp").astype(jnp.float32),
        lax.psum(grad_w_gate.astype(jnp.bfloat16), "dp").astype(jnp.float32),
        lax.psum(grad_w_up.astype(jnp.bfloat16), "dp").astype(jnp.float32),
        lax.psum(grad_w_down.astype(jnp.bfloat16), "dp").astype(jnp.float32),
    )
    return (
        output,
        grad_tokens,
        grad_norm_attn,
        grad_w_query,
        grad_w_key,
        grad_w_value,
        grad_w_out,
        grad_norm_mlp,
        grad_w_gate,
        grad_w_up,
        grad_w_down,
    )


def solution(mesh):
    in_specs = (
        P(("dp", "tensor"), None),
        P("dp"),
        P("dp"),
        P(),
        P(None, "tensor"),
        P(None, "tensor"),
        P(None, "tensor"),
        P("tensor", None),
        P(),
        P(None, "tensor"),
        P(None, "tensor"),
        P("tensor", None),
        P(("dp", "tensor"), None),
    )
    out_specs = (
        P(("dp", "tensor"), None),
        P(("dp", "tensor"), None),
        P(),
        P(None, "tensor"),
        P(None, "tensor"),
        P(None, "tensor"),
        P("tensor", None),
        P(),
        P(None, "tensor"),
        P(None, "tensor"),
        P("tensor", None),
    )
    return jax.shard_map(body, mesh=mesh, in_specs=in_specs, out_specs=out_specs, check_vma=False)
```

profile of v0, /device:TPU:0, one launch (start us, length us, event | category | flops | bytes accessed | tf_op | source)
XLA Modules:
  0.0 1461.6 jit_solution(5925052065785356915)
XLA Ops:
  15.7 46.3 %all-gather.5.cloned.1.call-done = bf16[2048,1536]{1,0:T(8,128)(2,1)} async-done(((bf16[512,1536]{1,0:T(8,128)(2,1)}), bf16[2048,1536]{1,0:T(8,128)(2,1)}) %all-gather.5.cloned.1.call-update) | async-done | bytes 6291472 | tf_op jit(solution)/shard_map/all_gather | solution.py:104
  89.8 66.6 %while.28 = (s32[]{:T(128)}, bf16[4,512,2,2,96]{1,4,3,2,0:T(8,128)(2,1)}, f32[4,2,2,512]{3,2,1,0:T(2,128)}, s32[4,512]{1,0:T(4,128)S(1)}, s32[2048]{0:T(1024)S(1...) while((s32[]{:T(128)}, ...), condition=%wide.region_4.5_spmd.clone, body=%wide.region_1.4_spmd.clone.sunk | while | flops 1664284672 | bytes 60117144 | solution.py:135
  167.2 99.1 %reduce-scatter.5.cloned.1.call-done = f32[512,1536]{1,0:T(8,128)} async-done(((f32[2048,1536]{1,0:T(8,128)}), f32[512,1536]{1,0:T(8,128)}) %reduce-scatter.5.cloned.1.call-update) | async-done | bytes 3145744 | tf_op jit(solution)/shard_map/reduce_scatter | solution.py:138
  273.0 45.9 %all-gather.7.cloned.1.call-done = bf16[2048,1536]{1,0:T(8,128)(2,1)} async-done(((bf16[512,1536]{1,0:T(8,128)(2,1)}), bf16[2048,1536]{1,0:T(8,128)(2,1)}) %all-gather.7.cloned.1.call-update) | async-done | bytes 6291472 | tf_op jit(solution)/shard_map/all_gather | solution.py:148
  318.9 12.6 fusion.74
  331.5 8.8 fusion.73
  340.3 26.4 %all-gather.9.cloned.1.call-done = bf16[2048,1536]{1,0:T(8,128)(2,1)} async-done(((bf16[512,1536]{1,0:T(8,128)(2,1)}), bf16[2048,1536]{1,0:T(8,128)(2,1)}) %all-gather.9.cloned.1.call-update) | async-done | bytes 6291472 | tf_op jit(solution)/shard_map/all_gather | solution.py:162
  366.8 18.8 %multiply_convert_fusion = (bf16[2048,1024]{1,0:T(8,128)(2,1)}, bf16[2048,1024]{1,0:T(8,128)(2,1)}, bf16[2048,1024]{1,0:T(8,128)(2,1)}) fusion(f32[2048,1024]{1,0:T(8,128)} %fusion.73, f32[2048,1024]{1,0:T(8,128)} %fusion.74, bf16[2048,1536]{1,0:T(8,128)(2,1)} %all-gather.9.cloned.1.call-done, bf16[1024,1536]{1,0:T(8,128)(2,1)S(1)} %copy-done), kind=kOutput, calls=%fused_computation.69 | convolution fusion | flops 6473908224 | bytes 38797312 | tf_op jit(solution)/shard_map/dot_general | solution.py:61
  385.6 11.6 fusion.75
  397.2 12.9 convolution_add_fusion
  410.1 99.1 %reduce-scatter.9.cloned.1.call-done = f32[512,1536]{1,0:T(8,128)} async-done(((f32[2048,1536]{1,0:T(8,128)}), f32[512,1536]{1,0:T(8,128)}) %reduce-scatter.9.cloned.1.call-update) | async-done | bytes 3145744 | tf_op jit(solution)/shard_map/reduce_scatter | solution.py:171
  517.6 46.5 %all-gather.11.cloned.1.call-done = bf16[2048,1536]{1,0:T(8,128)(2,1)} async-done(((bf16[512,1536]{1,0:T(8,128)(2,1)}), bf16[2048,1536]{1,0:T(8,128)(2,1)}) %all-gather.11.cloned.1.call-update) | async-done | bytes 6291472 | tf_op jit(solution)/shard_map/all_gather | solution.py:181
  584.7 274.0 %while.29 = (s32[]{:T(128)}, f32[2048,2,96]{0,2,1:T(8,128)}, f32[2048,2,96]{0,2,1:T(8,128)}, f32[4,512,2,2,96]{1,0,4,3,2:T(4,128)}, bf16[4,512,2,2,96]{1,4,3,2,0...) while((s32[]{:T(128)}, f32[2048,2,96]{0,2,1:T(8,128)}, ...), condition=%wide.region_12.13_spmd.clone, body=%wide.region_10.12_spmd.clone.sunk | while | flops 4094752768 | bytes 214511840 | solution.py:222
  603.6 12.6 fusion.155
  616.3 12.2 fusion.156
  636.6 16.1 %dynamic_update_slice.22 = f32[4,512,2,2,96]{1,0,4,3,2:T(4,128)} dynamic-update-slice(f32[4,512,2,2,96]{1,0,4,3,2:T(4,128)} %get-tuple-element.503, f32[1,512,2,2,96]{1,0,4,3,2:T(1,128)} %copy.49, s32[]{:T(128)S(6)} %copy.66, s32[]{:T(128)} %constant.58.clone.1..sunk, s32[]{:T(128)} %constant.58.clone.1..sunk, s32[]{:T(128)} %constant.58.clone.1..sunk, s32[]{:T(128)} %constant.58.clone.1..sunk) | dynamic-update-slice | bytes 1572868 | tf_op jit(solution)/shard_map/while/body/jit(dynamic_update_index_in_dim)/dynamic_update_slice | solution.py:222
  671.7 12.6 fusion.155
  684.3 12.2 fusion.156
  705.2 16.1 %dynamic_update_slice.22 = f32[4,512,2,2,96]{1,0,4,3,2:T(4,128)} dynamic-update-slice(f32[4,512,2,2,96]{1,0,4,3,2:T(4,128)} %get-tuple-element.503, f32[1,512,2,2,96]{1,0,4,3,2:T(1,128)} %copy.49, s32[]{:T(128)S(6)} %copy.66, s32[]{:T(128)} %constant.58.clone.1..sunk, s32[]{:T(128)} %constant.58.clone.1..sunk, s32[]{:T(128)} %constant.58.clone.1..sunk, s32[]{:T(128)} %constant.58.clone.1..sunk) | dynamic-update-slice | bytes 1572868 | tf_op jit(solution)/shard_map/while/body/jit(dynamic_update_index_in_dim)/dynamic_update_slice | solution.py:222
  740.3 12.6 fusion.155
  753.0 12.2 fusion.156
  773.8 16.1 %dynamic_update_slice.22 = f32[4,512,2,2,96]{1,0,4,3,2:T(4,128)} dynamic-update-slice(f32[4,512,2,2,96]{1,0,4,3,2:T(4,128)} %get-tuple-element.503, f32[1,512,2,2,96]{1,0,4,3,2:T(1,128)} %copy.49, s32[]{:T(128)S(6)} %copy.66, s32[]{:T(128)} %constant.58.clone.1..sunk, s32[]{:T(128)} %constant.58.clone.1..sunk, s32[]{:T(128)} %constant.58.clone.1..sunk, s32[]{:T(128)} %constant.58.clone.1..sunk) | dynamic-update-slice | bytes 1572868 | tf_op jit(solution)/shard_map/while/body/jit(dynamic_update_index_in_dim)/dynamic_update_slice | solution.py:222
  809.0 12.6 fusion.155
  821.6 12.2 fusion.156
  842.5 16.1 %dynamic_update_slice.22 = f32[4,512,2,2,96]{1,0,4,3,2:T(4,128)} dynamic-update-slice(f32[4,512,2,2,96]{1,0,4,3,2:T(4,128)} %get-tuple-element.503, f32[1,512,2,2,96]{1,0,4,3,2:T(1,128)} %copy.49, s32[]{:T(128)S(6)} %copy.66, s32[]{:T(128)} %constant.58.clone.1..sunk, s32[]{:T(128)} %constant.58.clone.1..sunk, s32[]{:T(128)} %constant.58.clone.1..sunk, s32[]{:T(128)} %constant.58.clone.1..sunk) | dynamic-update-slice | bytes 1572868 | tf_op jit(solution)/shard_map/while/body/jit(dynamic_update_index_in_dim)/dynamic_update_slice | solution.py:222
  883.0 12.8 add_convert_fusion
  895.9 10.9 convolution_convert_fusion
  906.9 12.0 convolution_convert_fusion.2
  919.0 10.1 convolution_convert_fusion.3
  957.3 40.1 %all-reduce = (f32[1536]{0:T(1024)}, f32[1536]{0:T(1024)}) all-reduce(f32[1536]{0:T(1024)S(1)} %get-tuple-element.234, f32[1536]{0:T(1024)S(1)} %copy-done.41), channel_id=1, replica_groups=mesh['dp'=8,'tensor'=4] {'dp','tensor'}, use_global_device_ids=true, to_apply=%region_16.17 | all-reduce | flops 3072 | bytes 24576 | tf_op jit(solution)/shard_map/psum | solution.py:254
  997.4 19.3 %reduce-scatter.7.cloned.1.call-done = bf16[512,1536]{1,0:T(8,128)(2,1)} async-done(((bf16[2048,1536]{1,0:T(8,128)(2,1)}), bf16[512,1536]{1,0:T(8,128)(2,1)}) %reduce-scatter.7.cloned.1.call-update) | async-done | bytes 1572880 | tf_op jit(solution)/shard_map/reduce_scatter | solution.py:155
  1023.7 413.4 %all-reduce.4.cloned.1.call-done = (bf16[1536,384]{1,0:T(8,128)(2,1)}, bf16[1536,192]{0,1:T(8,128)(2,1)}, bf16[1536,192]{0,1:T(8,128)(2,1)}, bf16[384,1536]{1,0:...) async-done(((bf16[1536,384]{1,0:T(8,128)(2,1)}, bf16[1536,192]{0,1:T(8,128)(2,1)}, bf16[1536,192]{0,1:T(8,128)(2,1)}, ...) | async-done | bytes 12976144 | tf_op jit(solution)/shard_map/psum | solution.py:256
  (276 shorter events, 335.2 us)
Async XLA Ops:
  7.2 359.6 %copy-start = (bf16[1024,1536]{1,0:T(8,128)(2,1)S(1)}, bf16[1024,1536]{1,0:T(8,128)(2,1)}, u32[]{:S(2)}) copy-start(bf16[1024,1536]{1,0:T(8,128)(2,1)} %param.28) | copy-start | bytes 9437188
  7.2 54.8 %all-gather.5.cloned.1.call-start = ((), (), s32[]{:S(2)}) async-start(), calls=%async_computation.4 | async-start | bytes 7864320 | tf_op jit(solution)/shard_map/all_gather | solution.py:104
  12.8 253.6 %reduce-scatter.5.cloned.1.call-start = ((), (), s32[]{:S(2)}) async-start(), calls=%async_computation.5 | async-start | bytes 15728640 | tf_op jit(solution)/shard_map/reduce_scatter | solution.py:138
  15.7 55.7 %copy-start.7 = (f32[2048,48]{0,1:T(8,128)}, f32[2048,48]{0,1:T(8,128)S(1)}, u32[]{:S(2)}) copy-start(f32[2048,48]{0,1:T(8,128)S(1)} %get-tuple-element.310) | copy-start | bytes 1179652
  167.2 103.7 %copy-start.35 = (f32[1536]{0:T(1024)S(1)}, f32[1536]{0:T(1024)}, u32[]{:S(2)}) copy-start(f32[1536]{0:T(1024)} %param.25) | copy-start | bytes 18436
  167.2 151.7 %all-gather.7.cloned.1.call-start = ((), (), s32[]{:S(2)}) async-start(), calls=%async_computation.6 | async-start | bytes 7864320 | tf_op jit(solution)/shard_map/all_gather | solution.py:148
  269.2 244.4 %copy-start.39 = (f32[512]{0:T(512)}, f32[512]{0:T(512)S(1)}, u32[]{:S(2)}) copy-start(f32[512]{0:T(512)S(1)} %add_rsqrt_fusion) | copy-start | bytes 6148
  272.4 94.4 %all-gather.9.cloned.1.call-start = ((), (), s32[]{:S(2)}) async-start(), calls=%async_computation.8 | async-start | bytes 7864320 | tf_op jit(solution)/shard_map/all_gather | solution.py:162
  273.0 236.3 %reduce-scatter.9.cloned.1.call-start = ((), (), s32[]{:S(2)}) async-start(), calls=%async_computation.9 | async-start | bytes 15728640 | tf_op jit(solution)/shard_map/reduce_scatter | solution.py:171
  318.9 12.6 copy-start.48
  318.9 12.6 copy-start.49
  366.8 18.8 %copy-start.50 = (bf16[1536,1024]{1,0:T(8,128)(2,1)S(1)}, bf16[1536,1024]{1,0:T(8,128)(2,1)}, u32[]{:S(2)}) copy-start(bf16[1536,1024]{1,0:T(8,128)(2,1)} %param.26) | copy-start | bytes 9437188
  385.5 11.6 copy-start.51
  385.5 11.6 copy-start.53
  410.1 154.0 %all-gather.11.cloned.1.call-start = ((), (), s32[]{:S(2)}) async-start(), calls=%async_computation.10 | async-start | bytes 7864320 | tf_op jit(solution)/shard_map/all_gather | solution.py:181
  517.5 436.8 %reduce-scatter.11.cloned.1.call-start = ((), (), s32[]{:S(2)}) async-start(), calls=%async_computation.11 | async-start | bytes 7864320 | tf_op jit(solution)/shard_map/reduce_scatter | solution.py:242
  616.2 12.2 copy-start.2
  684.3 12.2 copy-start.2
  753.0 12.2 copy-start.2
  821.6 12.2 copy-start.2
  868.4 14.7 %copy-start.20 = (bf16[2048,2,96]{0,2,1:T(8,128)(2,1)}, bf16[2048,2,96]{0,2,1:T(8,128)(2,1)S(1)}, u32[]{:S(2)}) copy-start(bf16[2048,2,96]{0,2,1:T(8,128)(2,1)S(1)} %convert_element_type.138) | copy-start | bytes 2359300
  895.8 120.9 %reduce-scatter.7.cloned.1.call-start = ((), (), s32[]{:S(2)}) async-start(), calls=%async_computation.7 | async-start | bytes 7864320 | tf_op jit(solution)/shard_map/reduce_scatter | solution.py:155
  906.8 530.3 %all-reduce.4.cloned.1.call-start = ((), (), s32[]{:S(2)}) async-start(), calls=%async_computation.12 | async-start | bytes 25952256 | tf_op jit(solution)/shard_map/psum | solution.py:256
  906.9 12.1 copy-start.52
  906.9 22.2 %slice-start.2 = ((s8[6291456]{0:T(1024)(128)(4,1)}), s8[4194304]{0:T(1024)(128)(4,1)S(1)}, s32[]{:S(2)}) async-start(s8[6291456]{0:T(1024)(128)(4,1)} %bitcast.262), calls=%async_computation.15 | async-start | bytes 8388608
  918.9 10.2 slice-start.3
  918.9 10.2 copy-start.54
  918.9 18.7 %slice-start = ((s8[6291456]{0:T(1024)(128)(4,1)}), s8[4194304]{0:T(1024)(128)(4,1)S(1)}, s32[]{:S(2)}) async-start(s8[6291456]{0:T(1024)(128)(4,1)} %bitcast.260), calls=%async_computation.13 | async-start | bytes 8388608
  929.1 8.6 copy-start.16
  950.4 66.3 %copy-start.36 = (f32[1536]{0:T(1024)S(1)}, f32[1536]{0:T(1024)}, u32[]{:S(2)}) copy-start(f32[1536]{0:T(1024)} %param.25) | copy-start | bytes 18436
  950.4 66.3 %copy-start.40 = (f32[512]{0:T(512)S(1)}, f32[512]{0:T(512)}, u32[]{:S(2)}) copy-start(f32[512]{0:T(512)} %copy-done.39) | copy-start | bytes 6148
  950.4 66.3 %copy-start.45 = (f32[512]{0:T(512)S(1)}, f32[512]{0:T(512)}, u32[]{:S(2)}) copy-start(f32[512]{0:T(512)} %copy-done.44) | copy-start | bytes 6148
  (47 other events, 204.7 us)
Sparse Core Ops, SparseCore 0:
  12.9 49.0 all-gather.4
  167.3 99.0 reduce-scatter.4
  272.5 46.3 all-gather.6
  320.3 46.3 all-gather.8
  410.2 99.0 reduce-scatter.8
  517.7 46.3 all-gather.10
  895.9 58.3 reduce-scatter.10
  957.6 59.0 reduce-scatter.6
  1023.5 413.5 all-reduce.3
where the time goes:
time: 1470 us; the launch traced here: 1460 us
  waiting for transfers between devices  801 us (54%)
  matrix products  336 us (23%)
  other arithmetic  136 us (9%)
  local copies, waits for them, and re-layouts  132 us (9%)
  blocking collectives  40.1 us (3%)
  between operations  14.9 us (1%)
    psum x1, waiting for transfers between devices, body(): lax.psum(grad_w_query.astype(jnp.bfloat16), 'dp').astype(jnp.float32)  413 us
    reduce_scatter x1, waiting for transfers between devices, body(): lax.psum_scatter(contract_cols(grad_gate, w_gate) + contract_cols(grad_up...  99.1 us
    reduce_scatter x1, waiting for transfers between devices, body(): lax.psum_scatter(jnp.dot(row_slice, w_out, preferred_element_type=jnp.flo...  99.1 us
    dot_general x7, matrix products, contract_cols(): lax.dot_general(left, right, (((1,), (1,)), ((), ())), preferred_element_...  76.6 us
    dynamic_update_slice x8, local copies, waits for them, and re-layouts, body(): lax.scan(attend_back, (zero_state, zero_state), (blocks_of_query, grad_bl...  71.2 us
    dot_general x4, matrix products, attend_back(): jnp.einsum('qgrd,kgd->grqk', grad_block, heads_of_value, preferred_elemen...  50.6 us
    convert_element_type x4, other arithmetic, attend_back(): grad_scores = (weights * (grad_weights - inner_sum)).astype(jnp.bfloat16)  48.7 us
    all_gather x1, waiting for transfers between devices, body(): lax.all_gather(grad_hidden_one.astype(jnp.bfloat16), 'tensor', axis=0, ti...  46.5 us
  transfers between devices with their start and end apart: 9, of which 9 were waited for; matrix products, arithmetic and copies ran while one was open for 6% of the time, Pallas kernels for 0%

commit v1 on v0

--- a/solution.py
+++ b/solution.py
@@ -101,7 +101,22 @@
     inverse_one = rms_inverse(inputs)
     unit_one = inputs * inverse_one
     first_normalized = (unit_one * norm_attn).astype(jnp.bfloat16)
-    attn_in = lax.all_gather(first_normalized, "tensor", axis=0, tiled=True)
+
+    def extend_field(my_tile, shard_axis, where_dim):
+        ndev = jax.lax.axis_size(shard_axis)
+        all_blocks = [(it, (it + 1) % ndev) for it in range(ndev)]
+
+        def _treat_frame(r_now):
+            if len(r_now) == ndev:
+                return r_now
+            return _treat_frame([jax.lax.ppermute(r_now[0], shard_axis, all_blocks), *r_now])
+
+        long_array = jnp.concatenate(_treat_frame([my_tile]), axis=where_dim)
+        return jnp.roll(
+            long_array, (jax.lax.axis_index(shard_axis) + 1) * my_tile.shape[where_dim], where_dim
+        )
+
+    attn_in = extend_field(first_normalized, "tensor", 0)
     query_proj = jnp.dot(attn_in, w_query, preferred_element_type=jnp.float32).reshape(
         sequence_length, q_heads, HEAD_SIZE
     )

time: 1470 us -> 1490 us (1.014)
    ppermute x0 -> x3, waiting for transfers between devices: none -> 58 us  [_treat_frame(): jax.lax.ppermute(r_now[0], shard_axis, all_blocks)]
    all_gather x1 -> x0, waiting for transfers between devices: 46.3 us -> none  [body(): attn_in = lax.all_gather(first_normalized, 'tensor', axis=0, tiled=True)]
  transfers between devices with their start and end apart: 9 -> 11, of which waited for: 9 -> 11; matrix products, arithmetic and copies ran while one was open for 6% -> 6% of each run, Pallas kernels for 0% -> 0%
where the time goes in v1:
time: 1490 us; the launch traced here: 1480 us
  waiting for transfers between devices  814 us (55%)
  matrix products  332 us (22%)
  local copies, waits for them, and re-layouts  145 us (10%)
  other arithmetic  135 us (9%)
  blocking collectives  40.1 us (3%)
  between operations  15.3 us (1%)
    psum x1, waiting for transfers between devices, body(): lax.psum(grad_w_query.astype(jnp.bfloat16), 'dp').astype(jnp.float32)  413 us
    reduce_scatter x1, waiting for transfers between devices, body(): lax.psum_scatter(jnp.dot(row_slice, w_out, preferred_element_type=jnp.flo...  101 us
    reduce_scatter x1, waiting for transfers between devices, body(): lax.psum_scatter(contract_cols(grad_gate, w_gate) + contract_cols(grad_up...  99.1 us
    dot_general x7, matrix products, contract_cols(): lax.dot_general(left, right, (((1,), (1,)), ((), ())), preferred_element_...  76.9 us
    dynamic_update_slice x8, local copies, waits for them, and re-layouts, body(): lax.scan(attend_back, (zero_state, zero_state), (blocks_of_query, grad_bl...  71.2 us
    ppermute x3, waiting for transfers between devices, _treat_frame(): jax.lax.ppermute(r_now[0], shard_axis, all_blocks)  58 us
    dot_general x4, matrix products, attend_back(): jnp.einsum('qgrd,kgd->grqk', grad_block, heads_of_value, preferred_elemen...  50.6 us
    convert_element_type x4, other arithmetic, attend_back(): grad_scores = (weights * (grad_weights - inner_sum)).astype(jnp.bfloat16)  48.7 us
  transfers between devices with their start and end apart: 11, of which 11 were waited for; matrix products, arithmetic and copies ran while one was open for 6% of the time, Pallas kernels for 0%

profile of v1, /device:TPU:0, one launch (start us, length us, event | category | flops | bytes accessed | tf_op | source)
XLA Modules:
  0.0 1482.9 jit_solution(6523914538570943360)
XLA Ops:
  11.6 20.0 %collective-permute-done = bf16[512,1536]{1,0:T(8,128)(2,1)S(1)} collective-permute-done((bf16[512,1536]{1,0:T(8,128)(2,1)S(1)}, bf16[512,1536]{1,0:T(8,128)(2,1)S(1)}, u32[]{:S(2)}, u32[]{:S(2)}) %collective-permute-start) | collective-permute-done | bytes 1572896 | tf_op jit(solution)/shard_map/ppermute | solution.py:112
  32.7 19.9 %collective-permute-done.1 = bf16[512,1536]{1,0:T(8,128)(2,1)} collective-permute-done((bf16[512,1536]{1,0:T(8,128)(2,1)S(1)}, bf16[512,1536]{1,0:T(8,128)(2,1)}, u32[]{:S(2)}, u32[]{:S(2)}) %collective-permute-start.1) | collective-permute-done | bytes 1572896 | tf_op jit(solution)/shard_map/ppermute | solution.py:112
  54.8 18.0 %collective-permute-done.2 = bf16[512,1536]{1,0:T(8,128)(2,1)} collective-permute-done((bf16[512,1536]{1,0:T(8,128)(2,1)}, bf16[512,1536]{1,0:T(8,128)(2,1)}, u32[]{:S(2)}, u32[]{:S(2)}) %collective-permute-start.2) | collective-permute-done | bytes 1572896 | tf_op jit(solution)/shard_map/ppermute | solution.py:112
  103.1 69.1 %while.28 = (s32[]{:T(128)}, bf16[4,512,2,2,96]{1,4,3,2,0:T(8,128)(2,1)}, f32[4,2,2,512]{3,2,1,0:T(2,128)}, s32[4,512]{1,0:T(4,128)S(1)}, s32[2048]{0:T(1024)S(1...) while((s32[]{:T(128)}, ...), condition=%wide.region_4.5_spmd.clone, body=%wide.region_1.4_spmd.clone.sunk | while | flops 1664284672 | bytes 60117144 | solution.py:150
  183.0 101.2 %reduce-scatter.5.cloned.1.call-done = f32[512,1536]{1,0:T(8,128)} async-done(((f32[2048,1536]{1,0:T(8,128)}), f32[512,1536]{1,0:T(8,128)}) %reduce-scatter.5.cloned.1.call-update) | async-done | bytes 3145744 | tf_op jit(solution)/shard_map/reduce_scatter | solution.py:153
  291.0 45.8 %all-gather.4.cloned.1.call-done = bf16[2048,1536]{1,0:T(8,128)(2,1)} async-done(((bf16[512,1536]{1,0:T(8,128)(2,1)}), bf16[2048,1536]{1,0:T(8,128)(2,1)}) %all-gather.4.cloned.1.call-update) | async-done | bytes 6291472 | tf_op jit(solution)/shard_map/all_gather | solution.py:163
  336.8 12.5 fusion.98
  358.2 26.6 %all-gather.6.cloned.1.call-done = bf16[2048,1536]{1,0:T(8,128)(2,1)} async-done(((bf16[512,1536]{1,0:T(8,128)(2,1)}), bf16[2048,1536]{1,0:T(8,128)(2,1)}) %all-gather.6.cloned.1.call-update) | async-done | bytes 6291472 | tf_op jit(solution)/shard_map/all_gather | solution.py:177
  384.8 18.9 %multiply_convert_fusion = (bf16[2048,1024]{1,0:T(8,128)(2,1)}, bf16[2048,1024]{1,0:T(8,128)(2,1)}, bf16[2048,1024]{1,0:T(8,128)(2,1)}) fusion(f32[2048,1024]{1,0:T(8,128)} %fusion.97, f32[2048,1024]{1,0:T(8,128)} %fusion.98, bf16[2048,1536]{1,0:T(8,128)(2,1)} %all-gather.6.cloned.1.call-done, bf16[1024,1536]{1,0:T(8,128)(2,1)S(1)} %copy-done), kind=kOutput, calls=%fused_computation.69 | convolution fusion | flops 6473908224 | bytes 38797312 | tf_op jit(solution)/shard_map/dot_general | solution.py:61
  403.7 11.8 fusion.99
  415.5 12.9 convolution_add_fusion
  428.4 99.1 %reduce-scatter.9.cloned.1.call-done = f32[512,1536]{1,0:T(8,128)} async-done(((f32[2048,1536]{1,0:T(8,128)}), f32[512,1536]{1,0:T(8,128)}) %reduce-scatter.9.cloned.1.call-update) | async-done | bytes 3145744 | tf_op jit(solution)/shard_map/reduce_scatter | solution.py:186
  535.9 46.5 %all-gather.8.cloned.1.call-done = bf16[2048,1536]{1,0:T(8,128)(2,1)} async-done(((bf16[512,1536]{1,0:T(8,128)(2,1)}), bf16[2048,1536]{1,0:T(8,128)(2,1)}) %all-gather.8.cloned.1.call-update) | async-done | bytes 6291472 | tf_op jit(solution)/shard_map/all_gather | solution.py:196
  603.0 276.7 %while.29 = (s32[]{:T(128)}, f32[2048,2,96]{0,2,1:T(8,128)}, f32[2048,2,96]{0,2,1:T(8,128)}, f32[4,512,2,2,96]{1,0,4,3,2:T(4,128)}, bf16[4,512,2,2,96]{1,4,3,2,0...) while((s32[]{:T(128)}, f32[2048,2,96]{0,2,1:T(8,128)}, ...), condition=%wide.region_12.13_spmd.clone, body=%wide.region_10.12_spmd.clone.sunk | while | flops 4094752768 | bytes 214511840 | solution.py:237
  622.6 12.7 fusion.173
  635.3 12.2 fusion.174
  655.6 16.1 %dynamic_update_slice.22 = f32[4,512,2,2,96]{1,0,4,3,2:T(4,128)} dynamic-update-slice(f32[4,512,2,2,96]{1,0,4,3,2:T(4,128)} %get-tuple-element.503, f32[1,512,2,2,96]{1,0,4,3,2:T(1,128)} %copy.49, s32[]{:T(128)S(6)} %copy.73, s32[]{:T(128)} %constant.81.clone.1..sunk, s32[]{:T(128)} %constant.81.clone.1..sunk, s32[]{:T(128)} %constant.81.clone.1..sunk, s32[]{:T(128)} %constant.81.clone.1..sunk) | dynamic-update-slice | bytes 1572868 | tf_op jit(solution)/shard_map/while/body/jit(dynamic_update_index_in_dim)/dynamic_update_slice | solution.py:237
  691.4 12.7 fusion.173
  704.0 12.2 fusion.174
  724.9 16.1 %dynamic_update_slice.22 = f32[4,512,2,2,96]{1,0,4,3,2:T(4,128)} dynamic-update-slice(f32[4,512,2,2,96]{1,0,4,3,2:T(4,128)} %get-tuple-element.503, f32[1,512,2,2,96]{1,0,4,3,2:T(1,128)} %copy.49, s32[]{:T(128)S(6)} %copy.73, s32[]{:T(128)} %constant.81.clone.1..sunk, s32[]{:T(128)} %constant.81.clone.1..sunk, s32[]{:T(128)} %constant.81.clone.1..sunk, s32[]{:T(128)} %constant.81.clone.1..sunk) | dynamic-update-slice | bytes 1572868 | tf_op jit(solution)/shard_map/while/body/jit(dynamic_update_index_in_dim)/dynamic_update_slice | solution.py:237
  760.7 12.7 fusion.173
  773.3 12.2 fusion.174
  794.2 16.1 %dynamic_update_slice.22 = f32[4,512,2,2,96]{1,0,4,3,2:T(4,128)} dynamic-update-slice(f32[4,512,2,2,96]{1,0,4,3,2:T(4,128)} %get-tuple-element.503, f32[1,512,2,2,96]{1,0,4,3,2:T(1,128)} %copy.49, s32[]{:T(128)S(6)} %copy.73, s32[]{:T(128)} %constant.81.clone.1..sunk, s32[]{:T(128)} %constant.81.clone.1..sunk, s32[]{:T(128)} %constant.81.clone.1..sunk, s32[]{:T(128)} %constant.81.clone.1..sunk) | dynamic-update-slice | bytes 1572868 | tf_op jit(solution)/shard_map/while/body/jit(dynamic_update_index_in_dim)/dynamic_update_slice | solution.py:237
  830.0 12.7 fusion.173
  842.6 12.2 fusion.174
  863.5 16.1 %dynamic_update_slice.22 = f32[4,512,2,2,96]{1,0,4,3,2:T(4,128)} dynamic-update-slice(f32[4,512,2,2,96]{1,0,4,3,2:T(4,128)} %get-tuple-element.503, f32[1,512,2,2,96]{1,0,4,3,2:T(1,128)} %copy.49, s32[]{:T(128)S(6)} %copy.73, s32[]{:T(128)} %constant.81.clone.1..sunk, s32[]{:T(128)} %constant.81.clone.1..sunk, s32[]{:T(128)} %constant.81.clone.1..sunk, s32[]{:T(128)} %constant.81.clone.1..sunk) | dynamic-update-slice | bytes 1572868 | tf_op jit(solution)/shard_map/while/body/jit(dynamic_update_index_in_dim)/dynamic_update_slice | solution.py:237
  904.1 12.8 add_convert_fusion
  916.9 10.9 convolution_convert_fusion
  927.9 12.0 convolution_convert_fusion.2
  978.3 40.1 %all-reduce = (f32[1536]{0:T(1024)}, f32[1536]{0:T(1024)}) all-reduce(f32[1536]{0:T(1024)S(1)} %get-tuple-element.234, f32[1536]{0:T(1024)S(1)} %copy-done.47), channel_id=1, replica_groups=mesh['dp'=8,'tensor'=4] {'dp','tensor'}, use_global_device_ids=true, to_apply=%region_16.17 | all-reduce | flops 3072 | bytes 24576 | tf_op jit(solution)/shard_map/psum | solution.py:269
  1018.4 19.4 %reduce-scatter.7.cloned.1.call-done = bf16[512,1536]{1,0:T(8,128)(2,1)} async-done(((bf16[2048,1536]{1,0:T(8,128)(2,1)}), bf16[512,1536]{1,0:T(8,128)(2,1)}) %reduce-scatter.7.cloned.1.call-update) | async-done | bytes 1572880 | tf_op jit(solution)/shard_map/reduce_scatter | solution.py:170
  1044.7 413.4 %all-reduce.4.cloned.1.call-done = (bf16[1536,384]{1,0:T(8,128)(2,1)}, bf16[1536,192]{0,1:T(8,128)(2,1)}, bf16[1536,192]{0,1:T(8,128)(2,1)}, bf16[384,1536]{1,0:...) async-done(((bf16[1536,384]{1,0:T(8,128)(2,1)}, bf16[1536,192]{0,1:T(8,128)(2,1)}, bf16[1536,192]{0,1:T(8,128)(2,1)}, ...) | async-done | bytes 12976144 | tf_op jit(solution)/shard_map/psum | solution.py:271
  (295 shorter events, 361.2 us)
Async XLA Ops:
  7.2 377.6 %copy-start = (bf16[1024,1536]{1,0:T(8,128)(2,1)S(1)}, bf16[1024,1536]{1,0:T(8,128)(2,1)}, u32[]{:S(2)}) copy-start(bf16[1024,1536]{1,0:T(8,128)(2,1)} %param.28) | copy-start | bytes 9437188
  7.2 45.5 %copy-start.31 = (s32[2048]{0:T(1024)S(1)}, s32[2048]{0:T(1024)}, u32[]{:S(2)}) copy-start(s32[2048]{0:T(1024)} %param.18) | copy-start | bytes 24580
  7.2 45.5 %copy-start.50 = (s32[2048]{0:T(1024)S(1)}, s32[2048]{0:T(1024)}, u32[]{:S(2)}) copy-start(s32[2048]{0:T(1024)} %param.19) | copy-start | bytes 24580
  7.2 277.0 %reduce-scatter.5.cloned.1.call-start = ((), (), s32[]{:S(2)}) async-start(), calls=%async_computation.4 | async-start | bytes 15728640 | tf_op jit(solution)/shard_map/reduce_scatter | solution.py:153
  9.2 70.6 %copy-start.43 = (f32[512]{0:T(512)}, f32[512]{0:T(512)S(1)}, u32[]{:S(2)}) copy-start(f32[512]{0:T(512)S(1)} %add_rsqrt_fusion.1) | copy-start | bytes 6148
  11.1 20.5 %collective-permute-start = (bf16[512,1536]{1,0:T(8,128)(2,1)S(1)}, bf16[512,1536]{1,0:T(8,128)(2,1)S(1)}, u32[]{:S(2)}, u32[]{:S(2)}) collective-permute-start(bf16[512,1536]{1,0:T(8,128)(2,1)S(1)} %fusion.65), channel_id=1, source_target_pairs={{0,1},{1,2},{2,3},{3,0},{4,5},{5,6},{6,7},{7,4},{8,9},{9,10},{10,1... | collective-permute-start | bytes 4718600 | tf_op jit(solution)/shard_map/ppermute | solution.py:112
  32.7 19.9 %collective-permute-start.1 = (bf16[512,1536]{1,0:T(8,128)(2,1)S(1)}, bf16[512,1536]{1,0:T(8,128)(2,1)}, u32[]{:S(2)}, u32[]{:S(2)}) collective-permute-start(bf16[512,1536]{1,0:T(8,128)(2,1)S(1)} %collective-permute-done), channel_id=1, source_target_pairs={{0,1},{1,2},{2,3},{3,0},{4,5},{5,6},{6,7},{7,4},{8,9},{9,10},{10,1... | collective-permute-start | bytes 4718600 | tf_op jit(solution)/shard_map/ppermute | solution.py:112
  52.7 20.2 %collective-permute-start.2 = (bf16[512,1536]{1,0:T(8,128)(2,1)}, bf16[512,1536]{1,0:T(8,128)(2,1)}, u32[]{:S(2)}, u32[]{:S(2)}) collective-permute-start(bf16[512,1536]{1,0:T(8,128)(2,1)} %collective-permute-done.1), channel_id=1, source_target_pairs={{0,1},{1,2},{2,3},{3,0},{4,5},{5,6},{6,7},{7,4},{8,9},{9,10},{10,1... | collective-permute-start | bytes 4718600 | tf_op jit(solution)/shard_map/ppermute | solution.py:112
  54.8 35.6 %copy-start.8 = (f32[2048,48]{0,1:T(8,128)}, f32[2048,48]{0,1:T(8,128)S(1)}, u32[]{:S(2)}) copy-start(f32[2048,48]{0,1:T(8,128)S(1)} %get-tuple-element.310) | copy-start | bytes 1179652
  54.8 35.6 %copy-start.10 = (f32[2048,48]{0,1:T(8,128)}, f32[2048,48]{0,1:T(8,128)S(1)}, u32[]{:S(2)}) copy-start(f32[2048,48]{0,1:T(8,128)S(1)} %get-tuple-element.311) | copy-start | bytes 1179652
  54.8 21.2 %copy-start.15 = (bf16[512,1536]{1,0:T(8,128)(2,1)S(1)}, bf16[512,1536]{1,0:T(8,128)(2,1)}, u32[]{:S(2)}) copy-start(bf16[512,1536]{1,0:T(8,128)(2,1)} %copy-done.14) | copy-start | bytes 4718596
  183.0 105.8 %copy-start.41 = (f32[1536]{0:T(1024)S(1)}, f32[1536]{0:T(1024)}, u32[]{:S(2)}) copy-start(f32[1536]{0:T(1024)} %param.25) | copy-start | bytes 18436
  183.0 153.8 %all-gather.4.cloned.1.call-start = ((), (), s32[]{:S(2)}) async-start(), calls=%async_computation.5 | async-start | bytes 7864320 | tf_op jit(solution)/shard_map/all_gather | solution.py:163
  287.1 244.8 %copy-start.45 = (f32[512]{0:T(512)}, f32[512]{0:T(512)S(1)}, u32[]{:S(2)}) copy-start(f32[512]{0:T(512)S(1)} %add_rsqrt_fusion) | copy-start | bytes 6148
  290.2 94.5 %all-gather.6.cloned.1.call-start = ((), (), s32[]{:S(2)}) async-start(), calls=%async_computation.7 | async-start | bytes 7864320 | tf_op jit(solution)/shard_map/all_gather | solution.py:177
  291.0 236.6 %reduce-scatter.9.cloned.1.call-start = ((), (), s32[]{:S(2)}) async-start(), calls=%async_computation.8 | async-start | bytes 15728640 | tf_op jit(solution)/shard_map/reduce_scatter | solution.py:186
  336.8 12.6 copy-start.51
  336.8 12.6 copy-start.52
  384.8 18.9 %copy-start.53 = (bf16[1536,1024]{1,0:T(8,128)(2,1)S(1)}, bf16[1536,1024]{1,0:T(8,128)(2,1)}, u32[]{:S(2)}) copy-start(bf16[1536,1024]{1,0:T(8,128)(2,1)} %param.26) | copy-start | bytes 9437188
  428.4 154.0 %all-gather.8.cloned.1.call-start = ((), (), s32[]{:S(2)}) async-start(), calls=%async_computation.9 | async-start | bytes 7864320 | tf_op jit(solution)/shard_map/all_gather | solution.py:196
  535.8 439.5 %reduce-scatter.11.cloned.1.call-start = ((), (), s32[]{:S(2)}) async-start(), calls=%async_computation.10 | async-start | bytes 7864320 | tf_op jit(solution)/shard_map/reduce_scatter | solution.py:257
  635.3 12.2 copy-start.2
  704.0 12.2 copy-start.2
  889.4 14.6 copy-start.23
  916.8 120.9 %reduce-scatter.7.cloned.1.call-start = ((), (), s32[]{:S(2)}) async-start(), calls=%async_computation.6 | async-start | bytes 7864320 | tf_op jit(solution)/shard_map/reduce_scatter | solution.py:170
  927.9 530.3 %all-reduce.4.cloned.1.call-start = ((), (), s32[]{:S(2)}) async-start(), calls=%async_computation.11 | async-start | bytes 25952256 | tf_op jit(solution)/shard_map/psum | solution.py:271
  927.9 22.3 %slice-start.3 = ((s8[6291456]{0:T(1024)(128)(4,1)}), s8[4194304]{0:T(1024)(128)(4,1)S(1)}, s32[]{:S(2)}) async-start(s8[6291456]{0:T(1024)(128)(4,1)} %bitcast.256), calls=%async_computation.15 | async-start | bytes 8388608
  940.0 18.9 %slice-start = ((s8[12582912]{0:T(1024)(128)(4,1)}), s8[4194304]{0:T(1024)(128)(4,1)S(1)}, s32[]{:S(2)}) async-start(s8[12582912]{0:T(1024)(128)(4,1)} %bitcast.254), calls=%async_computation.12 | async-start | bytes 8388608
  940.0 18.9 %slice-start.1 = ((s8[12582912]{0:T(1024)(128)(4,1)}), s8[4194304]{0:T(1024)(128)(4,1)S(1)}, s32[]{:S(2)}) async-start(s8[12582912]{0:T(1024)(128)(4,1)} %bitcast.254), calls=%async_computation.13 | async-start | bytes 8388608
  971.8 66.0 %copy-start.42 = (f32[1536]{0:T(1024)S(1)}, f32[1536]{0:T(1024)}, u32[]{:S(2)}) copy-start(f32[1536]{0:T(1024)} %param.25) | copy-start | bytes 18436
  971.8 66.0 %copy-start.46 = (f32[512]{0:T(512)S(1)}, f32[512]{0:T(512)}, u32[]{:S(2)}) copy-start(f32[512]{0:T(512)} %copy-done.45) | copy-start | bytes 6148
  971.8 65.9 %copy-start.49 = (f32[512]{0:T(512)S(1)}, f32[512]{0:T(512)}, u32[]{:S(2)}) copy-start(f32[512]{0:T(512)} %copy-done.48) | copy-start | bytes 6148
  (53 other events, 279.0 us)
Sparse Core Ops, SparseCore 0:
  183.1 101.1 reduce-scatter.4
  290.4 46.3 all-gather.3
  338.4 46.3 all-gather.5
  428.5 99.0 reduce-scatter.8
  536.0 46.3 all-gather.7
  917.0 58.3 reduce-scatter.10
  978.6 59.0 reduce-scatter.6
  1044.6 413.5 all-reduce.3
